TPU v7x, 128 devices: a whole 4x4x4 slice. The times are simulated.
128 devices in a mesh: seq: 32 (over x, y, core), head: 4 (over z).
Axes of the slice: x: 4, y: 4, z: 4, core: 2. Of those that a mesh axis runs over, the one named last changes fastest.
Arguments:
- tokens: bfloat16 [32768, 1536], P('seq', 'head'), may hold values from -6 to 6
- norm_gain: float32 [1536], replicated, may hold values from 0.1 to 1.9
- w_qkv: bfloat16 [1536, 4608], P(None, 'head'), may hold values from -0.15625 to 0.15625
- w_out: bfloat16 [1536, 1536], P('head'), may hold values from -0.15625 to 0.15625
- frame_ids: int32 [32, 16], P('seq'), may hold values from 0 to 7, never falling along the last dimension, each value on 1 to 4 neighbouring positions
- slot_gain: float32 [1536], replicated, may hold values from 0.1 to 1.9
- w_key: bfloat16 [1536, 256], replicated, may hold values from -0.15625 to 0.15625
- w_value: bfloat16 [1536, 256], replicated, may hold values from -0.15625 to 0.15625
- w_query: float32 [256, 256], replicated, may hold values from -0.375 to 0.375
- slot_init: float32 [64, 256], replicated, may hold values from -6 to 6
- w_input: float32 [256, 768], replicated, may hold values from -0.375 to 0.375
- w_hidden: float32 [256, 768], replicated, may hold values from -0.375 to 0.375
Outputs:
- mixed: bfloat16 [32768, 1536], P(('seq', 'head'))
- slots: float32 [64, 256], replicated
Inputs may be any that keep to these rules, and one draw needn't show every extreme that they name: `frame_ids`: ids never fall along a row; a frame covers 1 to 4 blocks, and in every row some frame covers exactly 4 blocks.
All inputs are finite; a program needn't handle non-finite values.
Results may differ from a plain program's by a relative error of at most 0.008.
Values may be sent and summed in bfloat16 or wider, within the bound.
A program may use at most 64 MiB of HBM per device.

v0:
```python
import jax
import jax.numpy as jnp
from jax import lax
from jax.sharding import PartitionSpec as P

HD = 64
ITERS = 3
BLK = 64


def layer_norm(values, gain):
    mean = jnp.mean(values, axis=-1, keepdims=True)
    centred = values - mean
    var = jnp.mean(centred * centred, axis=-1, keepdims=True)
    return centred * lax.rsqrt(var + 1e-06) * gain


def normalize_exp(scores):
    powers = jnp.exp(scores)
    return powers / jnp.sum(powers, axis=-1, keepdims=True)


def recurrent_cell(update, state, w_input, w_hidden):
    high = lax.Precision.HIGHEST
    width = state.shape[1]
    from_in = jnp.dot(update, w_input, precision=high)
    from_state = jnp.dot(state, w_hidden, precision=high)
    reset = jax.nn.sigmoid(from_in[:, :width] + from_state[:, :width])
    gate = jax.nn.sigmoid(from_in[:, width : 2 * width] + from_state[:, width : 2 * width])
    candidate = jnp.tanh(from_in[:, 2 * width :] + reset * from_state[:, 2 * width :])
    return (1.0 - gate) * candidate + gate * state


def local(
    tokens,
    norm_gain,
    w_qkv,
    w_out,
    frame_ids,
    slot_gain,
    w_key,
    w_value,
    w_query,
    slot_init,
    w_input,
    w_hidden,
):
    whole = lax.all_gather(tokens, "head", axis=1, tiled=True)
    tok_count = whole.shape[0]
    normed = layer_norm(whole.astype(jnp.float32), norm_gain).astype(jnp.bfloat16)
    qkv = jnp.dot(normed, w_qkv, preferred_element_type=jnp.float32).astype(jnp.bfloat16)
    heads_here = w_qkv.shape[1] // (3 * HD)
    split = jnp.transpose(qkv.reshape(tok_count, heads_here, 3, HD), (1, 0, 2, 3))
    tok_ids = jnp.repeat(frame_ids[0], BLK)
    same = tok_ids[:, None] == tok_ids[None, :]

    def one_head(head_qkv):
        scores = jnp.dot(
            head_qkv[:, 0, :], head_qkv[:, 1, :].T, preferred_element_type=jnp.float32
        ) * HD ** (-0.5)
        scores = jnp.where(same, scores, -jnp.inf)
        probs = normalize_exp(scores).astype(jnp.bfloat16)
        return jnp.dot(probs, head_qkv[:, 2, :], preferred_element_type=jnp.float32).astype(
            jnp.bfloat16
        )

    outputs = lax.map(one_head, split)
    attended = jnp.transpose(outputs, (1, 0, 2)).reshape(tok_count, heads_here * HD)
    own_rows = tok_count // lax.axis_size("head")
    own_start = lax.axis_index("head") * own_rows
    own = lax.dynamic_slice_in_dim(whole, own_start, own_rows, 0)
    projected = lax.psum_scatter(
        jnp.dot(attended, w_out, preferred_element_type=jnp.float32).astype(jnp.bfloat16),
        "head",
        scatter_dimension=0,
        tiled=True,
    ).astype(jnp.float32)
    mixed = (own.astype(jnp.float32) + projected).astype(jnp.bfloat16)
    slot_in = layer_norm(mixed.astype(jnp.float32), slot_gain).astype(jnp.bfloat16)
    keys = jnp.dot(slot_in, w_key, preferred_element_type=jnp.float32).astype(jnp.bfloat16)
    values = jnp.dot(slot_in, w_value, preferred_element_type=jnp.float32).astype(jnp.bfloat16)
    slots = slot_init
    width = slot_init.shape[1]
    ones = jnp.ones((width,), jnp.float32)
    for step in range(ITERS):
        query = jnp.dot(layer_norm(slots, ones), w_query, precision=lax.Precision.HIGHEST).astype(
            jnp.bfloat16
        )
        logits = jnp.dot(keys, query.T, preferred_element_type=jnp.float32) * width ** (-0.5)
        weights = normalize_exp(logits)
        numer = jnp.einsum(
            "ts,td->sd", weights.astype(jnp.bfloat16), values, preferred_element_type=jnp.float32
        )
        denom = jnp.sum(weights, axis=0)
        numer, denom = lax.psum((numer, denom), ("seq", "head"))
        slots = recurrent_cell(numer / denom[:, None], slots, w_input, w_hidden)
    return (mixed, slots)


def solution(mesh):
    placed = (
        P("seq", "head"),
        P(),
        P(None, "head"),
        P("head", None),
        P("seq", None),
        P(),
        P(),
        P(),
        P(),
        P(),
        P(),
        P(),
    )
    return jax.shard_map(
        local,
        mesh=mesh,
        in_specs=placed,
        out_specs=(P(("seq", "head"), None), P()),
        check_vma=False,
    )
```

profile of v0, /device:TPU:1, one launch (start us, length us, event | category | flops | bytes accessed | tf_op | source)
XLA Modules:
  0.0 575.2 jit_solution(1970555273158845083)
XLA Ops:
  9.0 43.7 %all-gather.2.cloned.1.call-done = bf16[1024,1536]{1,0:T(8,128)(2,1)} async-done(((bf16[1024,384]{1,0:T(8,128)(2,1)}), bf16[1024,1536]{1,0:T(8,128)(2,1)}) %all-gather.2.cloned.1.call-update) | async-done | bytes 3145744 | tf_op jit(solution)/shard_map/all_gather | solution.py:48
  52.7 2.5 convert_reduce_fusion
  56.5 5.8 %convolution_convert_fusion.1 = bf16[1024,1152]{1,0:T(8,128)(2,1)} fusion(bf16[1536,1152]{1,0:T(8,128)(2,1)S(1)} %copy-done, bf16[1024,1536]{1,0:T(8,128)(2,1)S(1)} %copy-done.1, f32[1536]{0:T(1024)S(1)} %copy-done.12, f32[1024]{0:T(1024)S(1)} %add_rsqrt_fusion, f32[1024]{0:T(1024)S(1)} %broadcast_multiply_fusion), kind=kOutput, calls=%fused_computation.23 | convolution fusion | flops 3632922624 | bytes 9058304 | tf_op jit(solution)/shard_map/dot_general | solution.py:51
  62.4 4.3 copy.15
  66.7 23.8 %while.11 = (s32[]{:T(128)}, bf16[6,1024,64]{1,2,0:T(8,128)(2,1)}, bf16[6,1024,3,64]{1,3,2,0:T(8,128)(2,1)}, s32[1024]{0:T(1024)S(1)}, s32[]{:T(128)}) while((s32[]{:T(128)}, bf16[6,1024,64]{1,2,0:T(8,128)(2,1)}, bf16[6,1024,3,64]{1,3,2,0:T(8,128)(2,1)}, s32[1024]{0:T(1024)S(1)}, s32[]{:T(128)}) %tuple.47), condition=%wide.region_4.5_spmd.clone, body=%wide.region_2.4_spmd.clone.sunk | while | flops 277937152 | bytes 9724481 | solution.py:67
  68.8 1.8 fusion.134
  72.8 1.8 fusion.134
  76.7 1.8 fusion.134
  80.7 1.8 fusion.134
  84.7 1.8 fusion.134
  88.6 1.8 fusion.134
  90.5 5.0 convolution_convert_fusion
  97.6 1.9 convolution_convert_fusion.6
  99.5 2.4 fusion.102
  102.0 32.3 %reduce-scatter.2.cloned.1.call-done = bf16[256,1536]{1,0:T(8,128)(2,1)} async-done(((bf16[1024,1536]{1,0:T(8,128)(2,1)}), bf16[256,1536]{1,0:T(8,128)(2,1)}) %reduce-scatter.2.cloned.1.call-update) | async-done | bytes 786448 | tf_op jit(solution)/shard_map/reduce_scatter | solution.py:72
  134.3 1.8 convert_reduce_fusion.1
  140.1 64.9 %psum.43 = f32[64]{0:T(128)S(1)} all-reduce(f32[64]{0:T(128)S(1)} %fusion.90), channel_id=1, replica_groups=mesh['seq'=32,'head'=4] {'seq','head'}, use_global_device_ids=true, to_apply=%region_13.14 | all-reduce | flops 64 | bytes 512 | tf_op jit(solution)/shard_map/psum | solution.py:95
  205.0 72.0 %all-reduce.4.cloned.1.call-done = f32[64,256]{1,0:T(8,128)} async-done(((f32[64,256]{1,0:T(8,128)}), f32[64,256]{1,0:T(8,128)}) %all-reduce.4.cloned.1.call-update) | async-done | bytes 65552 | tf_op jit(solution)/shard_map/psum | solution.py:95
  276.9 1.8 fusion.69
  279.9 2.4 fusion.103
  282.5 1.3 convolution_convert_fusion.5
  283.8 1.1 fusion.100
  287.3 63.8 %psum.45 = f32[64]{0:T(128)S(1)} all-reduce(f32[64]{0:T(128)S(1)} %fusion.91), channel_id=1, replica_groups=mesh['seq'=32,'head'=4] {'seq','head'}, use_global_device_ids=true, to_apply=%region_19.20 | all-reduce | flops 64 | bytes 512 | tf_op jit(solution)/shard_map/psum | solution.py:95
  351.1 69.9 %all-reduce.6.cloned.1.call-done = f32[64,256]{1,0:T(8,128)} async-done(((f32[64,256]{1,0:T(8,128)}), f32[64,256]{1,0:T(8,128)}) %all-reduce.6.cloned.1.call-update) | async-done | bytes 65552 | tf_op jit(solution)/shard_map/psum | solution.py:95
  421.1 1.8 fusion.66
  424.0 2.4 fusion.104
  426.7 1.3 convolution_convert_fusion.4
  427.9 1.1 fusion.101
  431.4 63.7 %psum.47 = f32[64]{0:T(128)S(1)} all-reduce(f32[64]{0:T(128)S(1)} %fusion.92), channel_id=1, replica_groups=mesh['seq'=32,'head'=4] {'seq','head'}, use_global_device_ids=true, to_apply=%region_25.26 | all-reduce | flops 64 | bytes 512 | tf_op jit(solution)/shard_map/psum | solution.py:95
  495.1 70.1 %all-reduce.8.cloned.1.call-done = f32[64,256]{1,0:T(8,128)} async-done(((f32[64,256]{1,0:T(8,128)}), f32[64,256]{1,0:T(8,128)}) %all-reduce.8.cloned.1.call-update) | async-done | bytes 65552 | tf_op jit(solution)/shard_map/psum | solution.py:95
  565.2 1.8 fusion.63
  567.0 1.6 fusion.30
  (86 shorter events, 29.2 us)
Async XLA Ops:
  7.2 49.4 %copy-start = (bf16[1536,1152]{1,0:T(8,128)(2,1)S(1)}, bf16[1536,1152]{1,0:T(8,128)(2,1)}, u32[]{:S(2)}) copy-start(bf16[1536,1152]{1,0:T(8,128)(2,1)} %param.16) | copy-start | bytes 10616836
  7.2 45.5 %all-gather.2.cloned.1.call-start = ((), (), s32[]{:S(2)}) async-start(), calls=%async_computation.1 | async-start | bytes 3932160 | tf_op jit(solution)/shard_map/all_gather | solution.py:48
  7.9 126.3 %reduce-scatter.2.cloned.1.call-start = ((), (), s32[]{:S(2)}) async-start(), calls=%async_computation.2 | async-start | bytes 3932160 | tf_op jit(solution)/shard_map/reduce_scatter | solution.py:72
  9.0 47.5 %copy-start.12 = (f32[1536]{0:T(1024)S(1)}, f32[1536]{0:T(1024)}, u32[]{:S(2)}) copy-start(f32[1536]{0:T(1024)} %param.15) | copy-start | bytes 18436
  52.7 2.8 copy-start.1
  95.5 40.9 %copy-start.13 = (f32[1536]{0:T(1024)S(1)}, f32[1536]{0:T(1024)}, u32[]{:S(2)}) copy-start(f32[1536]{0:T(1024)} %param.19) | copy-start | bytes 18436
  95.5 181.4 %all-reduce.4.cloned.1.call-start = ((), (), s32[]{:S(2)}) async-start(), calls=%async_computation.3 | async-start | bytes 131072 | tf_op jit(solution)/shard_map/psum | solution.py:95
  134.3 2.2 copy-start.10
  134.3 2.7 copy-start.11
  136.1 1.4 copy-start.2
  136.1 1.3 copy-start.9
  136.9 0.7 copy-start.5
  137.4 0.6 copy-start.14
  137.7 0.6 copy-start.6
  139.1 282.0 %all-reduce.6.cloned.1.call-start = ((), (), s32[]{:S(2)}) async-start(), calls=%async_computation.4 | async-start | bytes 131072 | tf_op jit(solution)/shard_map/psum | solution.py:95
  276.9 8.6 %copy-start.15 = (bf16[256,256]{1,0:T(8,128)(2,1)S(1)}, bf16[256,256]{1,0:T(8,128)(2,1)}, u32[]{:S(2)}) copy-start(bf16[256,256]{1,0:T(8,128)(2,1)} %copy-done.14) | copy-start | bytes 393220
  279.9 2.6 copy-start.3
  284.9 0.6 copy-start.7
  286.3 278.9 %all-reduce.8.cloned.1.call-start = ((), (), s32[]{:S(2)}) async-start(), calls=%async_computation.5 | async-start | bytes 131072 | tf_op jit(solution)/shard_map/psum | solution.py:95
  421.1 8.6 %copy-start.16 = (bf16[256,256]{1,0:T(8,128)(2,1)S(1)}, bf16[256,256]{1,0:T(8,128)(2,1)}, u32[]{:S(2)}) copy-start(bf16[256,256]{1,0:T(8,128)(2,1)} %copy-done.14) | copy-start | bytes 393220
  424.0 2.6 copy-start.4
  429.0 0.6 copy-start.8
Sparse Core Ops, SparseCore 0:
  9.7 42.9 all-gather.1
  95.7 38.5 reduce-scatter.1
  139.6 137.3 all-reduce.3
  286.4 134.5 all-reduce.5
  430.6 134.5 all-reduce.7
where the time goes:
time: 576 us; the launch traced here: 575 us
  waiting for transfers between devices  289 us (50%)
  blocking collectives  192 us (33%)
  matrix products  51.3 us (9%)
  other arithmetic  14.7 us (3%)
  between operations  14.1 us (2%)
  local copies, waits for them, and re-layouts  13.7 us (2%)
    psum x3, waiting for transfers between devices, local(): numer, denom = lax.psum((numer, denom), ('seq', 'head'))  212 us
    psum x3, blocking collectives, local(): numer, denom = lax.psum((numer, denom), ('seq', 'head'))  192 us
    all_gather x1, waiting for transfers between devices, local(): whole = lax.all_gather(tokens, 'head', axis=1, tiled=True)  43.7 us
    reduce_scatter x1, waiting for transfers between devices, local(): lax.psum_scatter(jnp.dot(attended, w_out, preferred_element_type=jnp.floa...  32.3 us
  transfers between devices with their start and end apart: 5, of which 5 were waited for; matrix products, arithmetic and copies ran while one was open for 2% of the time, Pallas kernels for 0%

commit v1 on v0

--- a/solution.py
+++ b/solution.py
@@ -92,7 +92,7 @@
             "ts,td->sd", weights.astype(jnp.bfloat16), values, preferred_element_type=jnp.float32
         )
         denom = jnp.sum(weights, axis=0)
-        numer, denom = lax.psum((numer, denom), ("seq", "head"))
+        numer, denom = lax.psum(lax.psum((numer, denom), "seq"), "head")
         slots = recurrent_cell(numer / denom[:, None], slots, w_input, w_hidden)
     return (mixed, slots)
 

time: 576 us -> 669 us (1.16)
  waiting for transfers between devices: 289 us -> 354 us
  blocking collectives: 192 us -> 214 us
    psum x3 -> x6, waiting for transfers between devices: 212 us -> 275 us  [local(): numer, denom = lax.psum(lax.psum((numer, denom), 'seq'), 'head')]
    psum x3 -> x6, blocking collectives: 192 us -> 214 us  [local(): numer, denom = lax.psum(lax.psum((numer, denom), 'seq'), 'head')]
  transfers between devices with their start and end apart: 5 -> 8, of which waited for: 5 -> 5; matrix products, arithmetic and copies ran while one was open for 2% -> 2% of each run, Pallas kernels for 0% -> 0%
where the time goes in v1:
time: 669 us; the launch traced here: 665 us
  waiting for transfers between devices  354 us (53%)
  blocking collectives  214 us (32%)
  matrix products  53.1 us (8%)
  other arithmetic  14.7 us (2%)
  local copies, waits for them, and re-layouts  14.5 us (2%)
  between operations  14.4 us (2%)
    psum x6, waiting for transfers between devices, local(): numer, denom = lax.psum(lax.psum((numer, denom), 'seq'), 'head')  275 us
    psum x6, blocking collectives, local(): numer, denom = lax.psum(lax.psum((numer, denom), 'seq'), 'head')  214 us
    all_gather x1, waiting for transfers between devices, local(): whole = lax.all_gather(tokens, 'head', axis=1, tiled=True)  43.7 us
    reduce_scatter x1, waiting for transfers between devices, local(): lax.psum_scatter(jnp.dot(attended, w_out, preferred_element_type=jnp.floa...  34.7 us
  transfers between devices with their start and end apart: 8, of which 5 were waited for; matrix products, arithmetic and copies ran while one was open for 2% of the time, Pallas kernels for 0%

profile of v1, /device:TPU:1, one launch (start us, length us, event | category | flops | bytes accessed | tf_op | source)
XLA Modules:
  0.0 664.6 jit_solution(14134468201963811499)
XLA Ops:
  9.0 43.7 %all-gather.2.cloned.1.call-done = bf16[1024,1536]{1,0:T(8,128)(2,1)} async-done(((bf16[1024,384]{1,0:T(8,128)(2,1)}), bf16[1024,1536]{1,0:T(8,128)(2,1)}) %all-gather.2.cloned.1.call-update) | async-done | bytes 3145744 | tf_op jit(solution)/shard_map/all_gather | solution.py:48
  52.7 2.5 convert_reduce_fusion
  56.5 5.8 convolution_convert_fusion.1
  62.4 4.3 copy.15
  66.7 23.8 %while.11 = (s32[]{:T(128)}, bf16[6,1024,64]{1,2,0:T(8,128)(2,1)}, bf16[6,1024,3,64]{1,3,2,0:T(8,128)(2,1)}, s32[1024]{0:T(1024)S(1)}, s32[]{:T(128)}) while((s32[]{:T(128)}, bf16[6,1024,64]{1,2,0:T(8,128)(2,1)}, bf16[6,1024,3,64]{1,3,2,0:T(8,128)(2,1)}, s32[1024]{0:T(1024)S(1)}, s32[]{:T(128)}) %tuple.53), condition=%wide.region_4.5_spmd.clone, body=%wide.region_2.4_spmd.clone.sunk | while | flops 277937152 | bytes 9724481 | solution.py:67
  68.8 1.8 fusion.134
  72.8 1.8 fusion.134
  76.7 1.8 fusion.134
  80.7 1.8 fusion.134
  84.7 1.8 fusion.134
  88.6 1.8 fusion.134
  90.5 5.0 convolution_convert_fusion
  97.6 1.9 convolution_convert_fusion.6
  99.5 34.7 %reduce-scatter.2.cloned.1.call-done = bf16[256,1536]{1,0:T(8,128)(2,1)} async-done(((bf16[1024,1536]{1,0:T(8,128)(2,1)}), bf16[256,1536]{1,0:T(8,128)(2,1)}) %reduce-scatter.2.cloned.1.call-update) | async-done | bytes 786448 | tf_op jit(solution)/shard_map/reduce_scatter | solution.py:72
  134.3 1.8 convert_reduce_fusion.1
  139.1 2.4 fusion.102
  141.6 92.9 %all-reduce.7.cloned.1.call-done = f32[64,256]{1,0:T(8,128)} async-done(((f32[64,256]{1,0:T(8,128)}), f32[64,256]{1,0:T(8,128)}) %all-reduce.7.cloned.1.call-update) | async-done | bytes 65552 | tf_op jit(solution)/shard_map/psum | solution.py:95
  235.5 62.4 %psum.86 = f32[64]{0:T(128)S(1)} all-reduce(f32[64]{0:T(128)S(1)} %fusion.90), channel_id=1, replica_groups=mesh['seq'=32,'head'=4] {'seq'}, use_global_device_ids=true, to_apply=%region_14.15 | all-reduce | flops 64 | bytes 512 | tf_op jit(solution)/shard_map/psum | solution.py:95
  297.9 8.8 %psum.87 = f32[64]{0:T(128)S(1)} all-reduce(f32[64]{0:T(128)S(1)} %psum.86), channel_id=1, replica_groups=mesh['seq'=32,'head'=4] {'head'}, use_global_device_ids=true, to_apply=%region_15.16 | all-reduce | flops 64 | bytes 512 | tf_op jit(solution)/shard_map/psum | solution.py:95
  306.6 1.8 fusion.69
  313.2 1.7 fusion.81
  314.9 2.4 fusion.103
  317.4 90.9 %all-reduce.11.cloned.1.call-done = f32[64,256]{1,0:T(8,128)} async-done(((f32[64,256]{1,0:T(8,128)}), f32[64,256]{1,0:T(8,128)}) %all-reduce.11.cloned.1.call-update) | async-done | bytes 65552 | tf_op jit(solution)/shard_map/psum | solution.py:95
  409.2 62.4 %psum.90 = f32[64]{0:T(128)S(1)} all-reduce(f32[64]{0:T(128)S(1)} %fusion.91), channel_id=1, replica_groups=mesh['seq'=32,'head'=4] {'seq'}, use_global_device_ids=true, to_apply=%region_22.23 | all-reduce | flops 64 | bytes 512 | tf_op jit(solution)/shard_map/psum | solution.py:95
  471.6 9.0 %psum.91 = f32[64]{0:T(128)S(1)} all-reduce(f32[64]{0:T(128)S(1)} %psum.90), channel_id=1, replica_groups=mesh['seq'=32,'head'=4] {'head'}, use_global_device_ids=true, to_apply=%region_23.24 | all-reduce | flops 64 | bytes 512 | tf_op jit(solution)/shard_map/psum | solution.py:95
  480.6 1.8 fusion.66
  487.1 1.7 fusion.76
  488.9 2.4 fusion.104
  491.3 90.9 %all-reduce.15.cloned.1.call-done = f32[64,256]{1,0:T(8,128)} async-done(((f32[64,256]{1,0:T(8,128)}), f32[64,256]{1,0:T(8,128)}) %all-reduce.15.cloned.1.call-update) | async-done | bytes 65552 | tf_op jit(solution)/shard_map/psum | solution.py:95
  583.2 62.4 %psum.94 = f32[64]{0:T(128)S(1)} all-reduce(f32[64]{0:T(128)S(1)} %fusion.92), channel_id=1, replica_groups=mesh['seq'=32,'head'=4] {'seq'}, use_global_device_ids=true, to_apply=%region_30.31 | all-reduce | flops 64 | bytes 512 | tf_op jit(solution)/shard_map/psum | solution.py:95
  645.6 8.8 %psum.95 = f32[64]{0:T(128)S(1)} all-reduce(f32[64]{0:T(128)S(1)} %psum.94), channel_id=1, replica_groups=mesh['seq'=32,'head'=4] {'head'}, use_global_device_ids=true, to_apply=%region_31.32 | all-reduce | flops 64 | bytes 512 | tf_op jit(solution)/shard_map/psum | solution.py:95
  654.3 1.8 fusion.63
  (94 shorter events, 35.0 us)
Async XLA Ops:
  7.2 49.4 %copy-start = (bf16[1536,1152]{1,0:T(8,128)(2,1)S(1)}, bf16[1536,1152]{1,0:T(8,128)(2,1)}, u32[]{:S(2)}) copy-start(bf16[1536,1152]{1,0:T(8,128)(2,1)} %param.16) | copy-start | bytes 10616836
  7.2 45.5 %all-gather.2.cloned.1.call-start = ((), (), s32[]{:S(2)}) async-start(), calls=%async_computation.1 | async-start | bytes 3932160 | tf_op jit(solution)/shard_map/all_gather | solution.py:48
  7.9 126.3 %reduce-scatter.2.cloned.1.call-start = ((), (), s32[]{:S(2)}) async-start(), calls=%async_computation.2 | async-start | bytes 3932160 | tf_op jit(solution)/shard_map/reduce_scatter | solution.py:72
  9.0 47.5 %copy-start.12 = (f32[1536]{0:T(1024)S(1)}, f32[1536]{0:T(1024)}, u32[]{:S(2)}) copy-start(f32[1536]{0:T(1024)} %param.15) | copy-start | bytes 18436
  52.7 2.8 copy-start.1
  95.5 40.9 %copy-start.13 = (f32[1536]{0:T(1024)S(1)}, f32[1536]{0:T(1024)}, u32[]{:S(2)}) copy-start(f32[1536]{0:T(1024)} %param.19) | copy-start | bytes 18436
  95.5 138.9 %all-reduce.7.cloned.1.call-start = ((), (), s32[]{:S(2)}) async-start(), calls=%async_computation.3 | async-start | bytes 131072 | tf_op jit(solution)/shard_map/psum | solution.py:95
  134.3 2.2 copy-start.10
  134.3 2.7 copy-start.11
  136.1 1.4 copy-start.2
  136.1 1.3 copy-start.9
  136.9 0.7 copy-start.5
  137.4 0.6 copy-start.14
  137.7 0.6 copy-start.6
  139.1 167.5 %all-reduce.9.cloned.1.call-start = ((), (), s32[]{:S(2)}) async-start(), calls=%async_computation.4 | async-start | bytes 131072 | tf_op jit(solution)/shard_map/psum | solution.py:95
  234.5 173.8 %all-reduce.11.cloned.1.call-start = ((), (), s32[]{:S(2)}) async-start(), calls=%async_computation.5 | async-start | bytes 131072 | tf_op jit(solution)/shard_map/psum | solution.py:95
  309.5 0.6 copy-start.3
  312.6 0.6 copy-start.7
  314.9 165.7 %all-reduce.13.cloned.1.call-start = ((), (), s32[]{:S(2)}) async-start(), calls=%async_computation.6 | async-start | bytes 131072 | tf_op jit(solution)/shard_map/psum | solution.py:95
  408.2 173.9 %all-reduce.15.cloned.1.call-start = ((), (), s32[]{:S(2)}) async-start(), calls=%async_computation.7 | async-start | bytes 131072 | tf_op jit(solution)/shard_map/psum | solution.py:95
  483.5 0.6 copy-start.4
  486.5 0.6 copy-start.8
  488.8 165.5 %all-reduce.17.cloned.1.call-start = ((), (), s32[]{:S(2)}) async-start(), calls=%async_computation.8 | async-start | bytes 131072 | tf_op jit(solution)/shard_map/psum | solution.py:95
Sparse Core Ops, SparseCore 0:
  9.7 42.9 all-gather.1
  95.7 38.5 reduce-scatter.1
  139.2 95.1 all-reduce.6
  236.7 37.7 all-reduce.8
  315.0 93.1 all-reduce.10
  410.5 37.7 all-reduce.12
  489.0 93.1 all-reduce.14
  584.6 37.7 all-reduce.16
